TPU v7x, 256 devices: a whole 4x4x8 slice. The times are simulated.
256 devices in a mesh: dp: 4 (over y), space: 64 (over z, x, core).
Axes of the slice: x: 4, y: 4, z: 8, core: 2. Of those that a mesh axis runs over, the one named last changes fastest.
Arguments:
- features: bfloat16 [4, 128, 8, 8, 8, 128], P('dp', 'space'), may hold values from -6 to 6
- occupancy: int32 [4, 128, 8, 8, 8], P('dp', 'space'), may hold values from 0 to 1
- neighbours: int32 [4, 128, 26], P('dp', 'space'), may hold values from -1 to 127, as said below
- weight: bfloat16 [27, 128, 128], replicated, may hold values from -0.109375 to 0.109375
- cotangent: bfloat16 [4, 128, 8, 8, 8, 128], P('dp', 'space'), may hold values from -6 to 6
Outputs:
- response: bfloat16 [4, 128, 8, 8, 8, 128], P('dp', 'space')
- grad_input: bfloat16 [4, 128, 8, 8, 8, 128], P('dp', 'space')
- grad_weight: float32 [3456, 128], P('space')
Inputs may be any that keep to these rules, and one draw needn't show every extreme that they name: `neighbours`: A scan's blocks sit in a coarse grid of 64 slabs along the first dimension, each one cell thick and 4 cells across; each slab holds exactly 2 blocks, numbered slab by slab and inside a slab in the Morton order of their cells, so block g lies in slab g // 2; entry o of block g names the block in the adjacent cell in direction o, or -1 if that cell is empty or outside the grid; the relation is symmetric.
All inputs are finite; a program needn't handle non-finite values.
Results may differ from a plain program's by a relative error of at most 0.001.
Values may be sent and summed in bfloat16 or wider, within the bound.
A program may use at most 64 MiB of HBM per device.

v0:
```python
import math
import jax
import jax.numpy as jnp
from jax import lax
from jax.sharding import PartitionSpec as P

directions = [
    (along_x, along_y, along_z)
    for along_x in (-1, 0, 1)
    for along_y in (-1, 0, 1)
    for along_z in (-1, 0, 1)
    if (along_x, along_y, along_z) != (0, 0, 0)
]
kernel_taps = [
    (along_x, along_y, along_z)
    for along_x in range(3)
    for along_y in range(3)
    for along_z in range(3)
]


def padded_2(block, sides, width):
    for axis, dim in sides:
        count = lax.axis_size(axis)
        forward = [(i, i + 1) for i in range(count - 1)]
        backward = [(target, source) for source, target in forward]
        low = lax.ppermute(
            lax.slice_in_dim(block, block.shape[dim] - width, None, axis=dim), axis, forward
        )
        high = lax.ppermute(lax.slice_in_dim(block, 0, width, axis=dim), axis, backward)
        block = jnp.concatenate([low, block, high], axis=dim)
    return block


def side_slices(offset, extent):
    chosen = []
    for stride in offset:
        if stride == 1:
            chosen.append(slice(extent - 1, extent))
        elif stride == -1:
            chosen.append(slice(0, 1))
        else:
            chosen.append(slice(0, extent))
    return tuple(chosen)


def rim_slices(offset, extent):
    chosen = []
    for stride in offset:
        if stride == 1:
            chosen.append(slice(extent + 1, extent + 2))
        elif stride == -1:
            chosen.append(slice(0, 1))
        else:
            chosen.append(slice(1, extent + 1))
    return tuple(chosen)


def end_planes(field):
    count = field.shape[0]
    extent = field.shape[1]
    return jnp.stack([field[:, 0], field[:, extent - 1]]).reshape(2, count, -1)


def fill_rims(field, arrived, links, position):
    count = field.shape[0]
    extent = field.shape[1]
    channels = field.shape[-1]
    zero_bf = jnp.zeros((), jnp.bfloat16)
    before = arrived[0].reshape(count, extent, extent, channels)
    after = arrived[3].reshape(count, extent, extent, channels)
    padded = jnp.pad(field, ((0, 0), (1, 1), (1, 1), (1, 1), (0, 0)))
    whole = (slice(None),)
    for slot_index, offset in enumerate(directions):
        opposite = tuple((-stride for stride in offset))
        if offset[0] == 0:
            source = field[whole + side_slices(opposite, extent)]
        elif offset[0] == -1:
            source = before[whole + side_slices(opposite[1:], extent)][:, None]
        else:
            source = after[whole + side_slices(opposite[1:], extent)][:, None]
        other = links[:, slot_index]
        local = other - (position + offset[0]) * count
        picked = jnp.take(source, jnp.clip(local, 0, count - 1), axis=0)
        picked = jnp.where((other >= 0)[:, None, None, None, None], picked, zero_bf)
        padded = padded.at[whole + rim_slices(offset, extent)].set(picked)
    return padded


def window_at(padded, start_x, start_y, start_z, extent, block_lo, block_hi):
    channels = padded.shape[-1]
    return padded[
        block_lo:block_hi,
        start_x : start_x + extent,
        start_y : start_y + extent,
        start_z : start_z + extent,
    ].reshape(-1, channels)


def forward_each(padded_x, flat_g, weight, extent):
    count = padded_x.shape[0]
    channels = padded_x.shape[-1]
    summed = jnp.zeros((count * extent**3, channels), jnp.float32)
    grads = []
    for number, (along_x, along_y, along_z) in enumerate(kernel_taps):
        window = window_at(padded_x, along_x, along_y, along_z, extent, 0, count)
        summed = summed + jnp.dot(window, weight[number], preferred_element_type=jnp.float32)
        grads.append(
            lax.dot_general(
                window, flat_g, (((0,), (0,)), ((), ())), preferred_element_type=jnp.float32
            )
        )
    return (summed, jnp.concatenate(grads, axis=0))


def backward_each(padded_g, weight, extent):
    count = padded_g.shape[0]
    channels = padded_g.shape[-1]
    summed = jnp.zeros((count * extent**3, channels), jnp.float32)
    for number, (along_x, along_y, along_z) in enumerate(kernel_taps):
        window = window_at(padded_g, 2 - along_x, 2 - along_y, 2 - along_z, extent, 0, count)
        summed = summed + lax.dot_general(
            window, weight[number], (((1,), (1,)), ((), ())), preferred_element_type=jnp.float32
        )
    return summed


def per_device(features, occupancy, neighbours, weight, cotangent):
    count = features.shape[1]
    extent = features.shape[2]
    channels = features.shape[-1]
    devices = lax.axis_size("space")
    scans_count = lax.axis_size("dp")
    position = lax.axis_index("space")
    zero_bf = jnp.zeros((), jnp.bfloat16)
    zero_f = jnp.zeros((), jnp.float32)
    active = occupancy[0][..., None] > 0
    masked = jnp.where(active, features[0], zero_bf)
    upstream = jnp.where(active, cotangent[0], zero_bf)
    links = neighbours[0]
    arrived_x = padded_2(end_planes(masked), (("space", 0),), 1)
    padded_x = fill_rims(masked, arrived_x, links, position)
    flat_g = upstream.reshape(-1, channels)
    forward_sum, kernel_grad = forward_each(padded_x, flat_g, weight, extent)
    response = jnp.where(
        active, forward_sum.reshape(count, extent, extent, extent, channels), zero_f
    ).astype(jnp.bfloat16)
    arrived_g = padded_2(end_planes(upstream), (("space", 0),), 1)
    padded_g = fill_rims(upstream, arrived_g, links, position)
    backward_sum = backward_each(padded_g, weight, extent)
    grad_input = jnp.where(
        active, backward_sum.reshape(count, extent, extent, extent, channels), zero_f
    ).astype(jnp.bfloat16)
    across_scans = lax.psum(kernel_grad, "dp")
    shard_rows = lax.psum_scatter(across_scans, "space", scatter_dimension=0, tiled=True)
    scale_factor = 1.0 / math.sqrt(scans_count * devices * count * extent**3)
    return (response[None], grad_input[None], shard_rows * scale_factor)


def solution(mesh):
    placed = (
        P("dp", "space", None, None, None, None),
        P("dp", "space", None, None, None),
        P("dp", "space", None),
        P(),
        P("dp", "space", None, None, None, None),
    )
    return jax.shard_map(
        per_device,
        mesh=mesh,
        in_specs=placed,
        out_specs=(
            P("dp", "space", None, None, None, None),
            P("dp", "space", None, None, None, None),
            P("space", None),
        ),
        check_vma=False,
    )
```

profile of v0, /device:TPU:6, one launch (start us, length us, event | category | flops | bytes accessed | tf_op | source)
XLA Modules:
  0.0 260.6 jit_solution(3344975392172040905)
XLA Ops:
  1.5 1.2 bitcast_select_fusion
  2.8 1.9 collective-permute-start
  4.7 3.8 %collective-permute-start.2 = (bf16[1,2,8192]{2,1,0:T(2,128)(2,1)S(1)}, bf16[1,2,8192]{2,1,0:T(2,128)(2,1)S(1)}, u32[]{:S(2)}, u32[]{:S(2)}) collective-permute-start(bf16[1,2,8192]{2,1,0:T(2,128)(2,1)S(1)} %slice.2775), channel_id=1, source_target_pairs={{0,1},{1,2},{2,3},{3,4},{4,5},{5,6},{6,7},{7,8},{8,9},{9,10},{10,1... | collective-permute-start | bytes 98312 | tf_op jit(solution)/shard_map/ppermute | solution.py:27
  8.6 1.9 collective-permute-start.3
  10.5 2.2 collective-permute-start.1
  12.8 1.2 compare_reduce_fusion.19
  14.0 1.9 compare_reduce_fusion
  61.0 1.4 scatter.194
  62.4 1.4 scatter.195
  71.6 0.9 fusion.26
  72.5 0.9 fusion.25
  74.3 0.9 fusion.23
  75.2 0.9 fusion.22
  77.9 0.9 fusion.19
  79.7 0.9 fusion.17
  80.6 0.9 fusion.16
  82.4 0.9 fusion.14
  83.3 0.9 fusion.13
  84.2 0.9 fusion.12
  85.2 0.9 fusion.11
  86.1 0.9 fusion.10
  87.9 0.9 fusion.8
  90.6 0.9 fusion.5
  91.5 0.9 fusion.4
  93.3 0.9 fusion.2
  95.1 64.4 %fusion = f32[64,128]{1,0:T(8,128)S(1)} fusion(f32[3456,128]{1,0:T(8,128)} %fusion.1), kind=kCustom, calls=%all-reduce-scatter | all-reduce-scatter fusion | flops 524289 | bytes 1803264
  160.1 1.9 collective-permute-start.10
  162.0 4.2 %collective-permute-start.11 = (f32[64,128]{1,0:T(8,128)S(1)}, f32[64,128]{1,0:T(8,128)}, u32[]{:S(2)}, u32[]{:S(2)}) collective-permute-start(f32[64,128]{1,0:T(8,128)S(1)} %fusion), channel_id=1, source_target_pairs={{0,8},{1,9},{2,10},{3,11},{4,12},{5,13},{6,14},{7,15},{8,16},{9,17... | collective-permute-start | bytes 98312
  166.2 3.0 %collective-permute-start.12 = (f32[64,128]{1,0:T(8,128)S(1)}, f32[64,128]{1,0:T(8,128)}, u32[]{:S(2)}, u32[]{:S(2)}) collective-permute-start(f32[64,128]{1,0:T(8,128)S(1)} %fusion), channel_id=1, source_target_pairs={{0,9},{1,10},{2,11},{3,12},{4,13},{5,14},{6,15},{7,16},{8,17},{9,1... | collective-permute-start | bytes 98312
  169.2 3.3 %collective-permute-start.4 = (f32[64,128]{1,0:T(8,128)S(1)}, f32[64,128]{1,0:T(8,128)}, u32[]{:S(2)}, u32[]{:S(2)}) collective-permute-start(f32[64,128]{1,0:T(8,128)S(1)} %fusion), channel_id=1, source_target_pairs={{0,1},{1,2},{2,3},{3,4},{4,5},{5,6},{6,7},{7,8},{8,9},{9,10},{10,1... | collective-permute-start | bytes 98312
  172.5 1.4 fusion.184
  173.9 2.3 fusion.183
  179.1 0.9 scatter.224
  184.6 2.0 scatter.236
  186.7 2.0 scatter.239
  189.5 0.9 scatter.241
  194.1 0.9 scatter.251
  198.3 1.0 fusion.181
  199.3 3.9 %collective-permute-start.13 = (f32[54,128]{1,0:T(8,128)S(1)}, f32[54,128]{1,0:T(8,128)S(1)}, u32[]{:S(2)}, u32[]{:S(2)}) collective-permute-start(f32[54,128]{1,0:T(8,128)S(1)} %copy-done.22), channel_id=1, source_target_pairs={{0,10},{1,11},{2,12},{3,13},{4,14},{5,15},{6,16},{7,17},{8,18},{9,... | collective-permute-start | bytes 82952
  217.4 3.4 %collective-permute-start.5 = (f32[64,128]{1,0:T(8,128)S(1)}, f32[64,128]{1,0:T(8,128)S(1)}, u32[]{:S(2)}, u32[]{:S(2)}) collective-permute-start(f32[64,128]{1,0:T(8,128)S(1)} %fusion), channel_id=1, source_target_pairs={{0,2},{1,3},{2,4},{3,5},{4,6},{5,7},{6,8},{7,9},{8,10},{9,11},{10,... | collective-permute-start | bytes 98312
  220.9 2.6 collective-permute-start.6
  223.4 4.2 %collective-permute-start.7 = (f32[64,128]{1,0:T(8,128)S(1)}, f32[64,128]{1,0:T(8,128)S(1)}, u32[]{:S(2)}, u32[]{:S(2)}) collective-permute-start(f32[64,128]{1,0:T(8,128)S(1)} %fusion), channel_id=1, source_target_pairs={{0,4},{1,5},{2,6},{3,7},{4,8},{5,9},{6,10},{7,11},{8,12},{9,13},{1... | collective-permute-start | bytes 98312
  227.7 3.8 %collective-permute-start.8 = (f32[64,128]{1,0:T(8,128)S(1)}, f32[64,128]{1,0:T(8,128)S(1)}, u32[]{:S(2)}, u32[]{:S(2)}) collective-permute-start(f32[64,128]{1,0:T(8,128)S(1)} %fusion), channel_id=1, source_target_pairs={{0,5},{1,6},{2,7},{3,8},{4,9},{5,10},{6,11},{7,12},{8,13},{9,14},{... | collective-permute-start | bytes 98312
  231.5 1.9 collective-permute-start.9
  233.5 1.0 select_convert_fusion
  234.5 4.0 %collective-permute-done.9 = f32[64,128]{1,0:T(8,128)S(1)} collective-permute-done((f32[64,128]{1,0:T(8,128)S(1)}, f32[64,128]{1,0:T(8,128)S(1)}, u32[]{:S(2)}, u32[]{:S(2)}) %collective-permute-start.9) | collective-permute-done | bytes 32800
  238.6 4.2 %concatenate.156 = f32[694,128]{1,0:T(8,128)S(1)} concatenate(f32[54,128]{1,0:T(8,128)S(1)} %collective-permute-done.13, f32[64,128]{1,0:T(8,128)} %collective-permute-done.12, f32[64,128]{1,0:T(8,128)} %collective-permute-done.11, f32[64,128]{1,0:T(8,128)} %collective-permute-done.10, f32[64,128]{1,0:T(8,128)S(1)} %collective-permute-done.9, ...), dimensions={0} | concatenate | bytes 710656
  242.8 17.2 %psum.8 = f32[54,128]{1,0:T(8,128)S(1)} all-reduce(f32[54,128]{1,0:T(8,128)S(1)} %constant_dynamic-slice_fusion), channel_id=1, replica_groups=mesh['dp'=4,'space'=64] {'dp'}, use_global_device_ids=true, to_apply=%region_0.8 | all-reduce | flops 6912 | bytes 55296 | tf_op jit(solution)/shard_map/psum | solution.py:154
  (364 shorter events, 91.6 us)
Async XLA Ops:
  0.6 15.6 %copy-start.1 = (s32[1,2,26]{2,1,0:T(2,128)S(1)}, s32[1,2,26]{2,1,0:T(2,128)}, u32[]{:S(2)}) copy-start(s32[1,2,26]{2,1,0:T(2,128)} %param.125) | copy-start | bytes 628
  2.8 30.8 %collective-permute-start = (bf16[1,2,8192]{2,1,0:T(2,128)(2,1)S(1)}, bf16[1,2,8192]{2,1,0:T(2,128)(2,1)S(1)}, u32[]{:S(2)}, u32[]{:S(2)}) collective-permute-start(bf16[1,2,8192]{2,1,0:T(2,128)(2,1)S(1)} %slice.2668), channel_id=1, source_target_pairs={{0,1},{1,2},{2,3},{3,4},{4,5},{5,6},{6,7},{7,8},{8,9},{9,10},{10,1... | collective-permute-start | bytes 98312 | tf_op jit(solution)/shard_map/ppermute | solution.py:27
  4.7 28.8 %collective-permute-start.2 = (bf16[1,2,8192]{2,1,0:T(2,128)(2,1)S(1)}, bf16[1,2,8192]{2,1,0:T(2,128)(2,1)S(1)}, u32[]{:S(2)}, u32[]{:S(2)}) collective-permute-start(bf16[1,2,8192]{2,1,0:T(2,128)(2,1)S(1)} %slice.2775), channel_id=1, source_target_pairs={{0,1},{1,2},{2,3},{3,4},{4,5},{5,6},{6,7},{7,8},{8,9},{9,10},{10,1... | collective-permute-start | bytes 98312 | tf_op jit(solution)/shard_map/ppermute | solution.py:27
  8.6 25.1 %collective-permute-start.3 = (bf16[1,2,8192]{2,1,0:T(2,128)(2,1)S(1)}, bf16[1,2,8192]{2,1,0:T(2,128)(2,1)S(1)}, u32[]{:S(2)}, u32[]{:S(2)}) collective-permute-start(bf16[1,2,8192]{2,1,0:T(2,128)(2,1)S(1)} %slice.2793), channel_id=1, source_target_pairs={{1,0},{2,1},{3,2},{4,3},{5,4},{6,5},{7,6},{8,7},{9,8},{10,9},{11,1... | collective-permute-start | bytes 98312 | tf_op jit(solution)/shard_map/ppermute | solution.py:30
  10.5 23.1 %collective-permute-start.1 = (bf16[1,2,8192]{2,1,0:T(2,128)(2,1)S(1)}, bf16[1,2,8192]{2,1,0:T(2,128)(2,1)S(1)}, u32[]{:S(2)}, u32[]{:S(2)}) collective-permute-start(bf16[1,2,8192]{2,1,0:T(2,128)(2,1)S(1)} %slice.2703), channel_id=1, source_target_pairs={{1,0},{2,1},{3,2},{4,3},{5,4},{6,5},{7,6},{8,7},{9,8},{10,9},{11,1... | collective-permute-start | bytes 98312 | tf_op jit(solution)/shard_map/ppermute | solution.py:30
  22.2 10.1 %copy-start.23 = (u32[256]{0:T(256)S(1)}, u32[256]{0:T(256)}, u32[]{:S(2)}) copy-start(u32[256]{0:T(256)} %constant.1500) | copy-start | bytes 3076
  160.1 60.7 %collective-permute-start.10 = (f32[64,128]{1,0:T(8,128)S(1)}, f32[64,128]{1,0:T(8,128)}, u32[]{:S(2)}, u32[]{:S(2)}) collective-permute-start(f32[64,128]{1,0:T(8,128)S(1)} %fusion), channel_id=1, source_target_pairs={{0,7},{1,8},{2,9},{3,10},{4,11},{5,12},{6,13},{7,14},{8,15},{9,16}... | collective-permute-start | bytes 98312
  162.0 61.4 %collective-permute-start.11 = (f32[64,128]{1,0:T(8,128)S(1)}, f32[64,128]{1,0:T(8,128)}, u32[]{:S(2)}, u32[]{:S(2)}) collective-permute-start(f32[64,128]{1,0:T(8,128)S(1)} %fusion), channel_id=1, source_target_pairs={{0,8},{1,9},{2,10},{3,11},{4,12},{5,13},{6,14},{7,15},{8,16},{9,17... | collective-permute-start | bytes 98312
  166.2 61.4 %collective-permute-start.12 = (f32[64,128]{1,0:T(8,128)S(1)}, f32[64,128]{1,0:T(8,128)}, u32[]{:S(2)}, u32[]{:S(2)}) collective-permute-start(f32[64,128]{1,0:T(8,128)S(1)} %fusion), channel_id=1, source_target_pairs={{0,9},{1,10},{2,11},{3,12},{4,13},{5,14},{6,15},{7,16},{8,17},{9,1... | collective-permute-start | bytes 98312
  169.2 62.3 %collective-permute-start.4 = (f32[64,128]{1,0:T(8,128)S(1)}, f32[64,128]{1,0:T(8,128)}, u32[]{:S(2)}, u32[]{:S(2)}) collective-permute-start(f32[64,128]{1,0:T(8,128)S(1)} %fusion), channel_id=1, source_target_pairs={{0,1},{1,2},{2,3},{3,4},{4,5},{5,6},{6,7},{7,8},{8,9},{9,10},{10,1... | collective-permute-start | bytes 98312
  198.3 1.0 copy-start.22
  198.3 4.9 %copy-start = (bf16[27,128,128]{2,1,0:T(8,128)(2,1)S(1)}, bf16[27,128,128]{2,1,0:T(8,128)(2,1)}, u32[]{:S(2)}) copy-start(bf16[27,128,128]{2,1,0:T(8,128)(2,1)} %param.126) | copy-start | bytes 2654212
  199.3 4.4 %copy-start.21 = (bf16[2,8,8,8,128]{4,3,2,1,0:T(8,128)(2,1)S(1)}, bf16[2,8,8,8,128]{4,3,2,1,0:T(8,128)(2,1)}, u32[]{:S(2)}) copy-start(bf16[2,8,8,8,128]{4,3,2,1,0:T(8,128)(2,1)} %get-tuple-element.738) | copy-start | bytes 786436
  199.3 4.6 %copy-start.20 = (bf16[2,8,8,8,128]{4,3,2,1,0:T(8,128)(2,1)S(1)}, bf16[2,8,8,8,128]{4,3,2,1,0:T(8,128)(2,1)}, u32[]{:S(2)}) copy-start(bf16[2,8,8,8,128]{4,3,2,1,0:T(8,128)(2,1)} %get-tuple-element.737) | copy-start | bytes 786436
  199.3 18.1 %collective-permute-start.13 = (f32[54,128]{1,0:T(8,128)S(1)}, f32[54,128]{1,0:T(8,128)S(1)}, u32[]{:S(2)}, u32[]{:S(2)}) collective-permute-start(f32[54,128]{1,0:T(8,128)S(1)} %copy-done.22), channel_id=1, source_target_pairs={{0,10},{1,11},{2,12},{3,13},{4,14},{5,15},{6,16},{7,17},{8,18},{9,... | collective-permute-start | bytes 82952
  203.4 1.0 copy-start.19
  203.7 1.0 copy-start.18
  203.9 1.0 copy-start.17
  204.4 1.0 copy-start.16
  204.6 1.0 copy-start.15
  204.9 1.0 copy-start.14
  205.4 1.0 copy-start.13
  205.6 1.0 copy-start.12
  205.9 1.0 copy-start.11
  206.4 1.0 copy-start.10
  206.6 1.0 copy-start.9
  206.9 1.0 copy-start.8
  207.3 1.0 copy-start.7
  207.6 1.0 copy-start.6
  207.9 1.0 copy-start.5
  208.3 1.0 copy-start.4
  208.6 1.0 copy-start.3
  208.9 1.0 copy-start.2
  217.4 17.0 %collective-permute-start.5 = (f32[64,128]{1,0:T(8,128)S(1)}, f32[64,128]{1,0:T(8,128)S(1)}, u32[]{:S(2)}, u32[]{:S(2)}) collective-permute-start(f32[64,128]{1,0:T(8,128)S(1)} %fusion), channel_id=1, source_target_pairs={{0,2},{1,3},{2,4},{3,5},{4,6},{5,7},{6,8},{7,9},{8,10},{9,11},{10,... | collective-permute-start | bytes 98312
  220.9 13.6 %collective-permute-start.6 = (f32[64,128]{1,0:T(8,128)S(1)}, f32[64,128]{1,0:T(8,128)S(1)}, u32[]{:S(2)}, u32[]{:S(2)}) collective-permute-start(f32[64,128]{1,0:T(8,128)S(1)} %fusion), channel_id=1, source_target_pairs={{0,3},{1,4},{2,5},{3,6},{4,7},{5,8},{6,9},{7,10},{8,11},{9,12},{10... | collective-permute-start | bytes 98312
  223.4 11.1 %collective-permute-start.7 = (f32[64,128]{1,0:T(8,128)S(1)}, f32[64,128]{1,0:T(8,128)S(1)}, u32[]{:S(2)}, u32[]{:S(2)}) collective-permute-start(f32[64,128]{1,0:T(8,128)S(1)} %fusion), channel_id=1, source_target_pairs={{0,4},{1,5},{2,6},{3,7},{4,8},{5,9},{6,10},{7,11},{8,12},{9,13},{1... | collective-permute-start | bytes 98312
  227.7 6.8 %collective-permute-start.8 = (f32[64,128]{1,0:T(8,128)S(1)}, f32[64,128]{1,0:T(8,128)S(1)}, u32[]{:S(2)}, u32[]{:S(2)}) collective-permute-start(f32[64,128]{1,0:T(8,128)S(1)} %fusion), channel_id=1, source_target_pairs={{0,5},{1,6},{2,7},{3,8},{4,9},{5,10},{6,11},{7,12},{8,13},{9,14},{... | collective-permute-start | bytes 98312
  231.5 7.0 %collective-permute-start.9 = (f32[64,128]{1,0:T(8,128)S(1)}, f32[64,128]{1,0:T(8,128)S(1)}, u32[]{:S(2)}, u32[]{:S(2)}) collective-permute-start(f32[64,128]{1,0:T(8,128)S(1)} %fusion), channel_id=1, source_target_pairs={{0,6},{1,7},{2,8},{3,9},{4,10},{5,11},{6,12},{7,13},{8,14},{9,15},... | collective-permute-start | bytes 98312
where the time goes:
time: 263 us; the launch traced here: 261 us
  blocking collectives  81.5 us (31%)
  local copies, waits for them, and re-layouts  68.6 us (26%)
  starting transfers between devices  42.1 us (16%)
  matrix products  36.2 us (14%)
  other arithmetic  25.1 us (10%)
  waiting for transfers between devices  4.08 us (2%)
  between operations  3 us (1%)
    unnamed x1, blocking collectives  64.4 us
    unnamed x10, starting transfers between devices  32.2 us
    gather x52, local copies, waits for them, and re-layouts, fill_rims(): picked = jnp.take(source, jnp.clip(local, 0, count - 1), axis=0)  29.1 us
    scatter x52, local copies, waits for them, and re-layouts, fill_rims(): padded = padded.at[whole + rim_slices(offset, extent)].set(picked)  25.9 us
    dot_general x27, matrix products, forward_each(): lax.dot_general(window, flat_g, (((0,), (0,)), ((), ())), preferred_eleme...  24.4 us
    psum x1, blocking collectives, per_device(): across_scans = lax.psum(kernel_grad, 'dp')  17.2 us
    select_n x26, other arithmetic, fill_rims(): picked = jnp.where((other >= 0)[:, None, None, None, None], picked, zero_bf)  17.2 us
    unnamed x68, local copies, waits for them, and re-layouts  7.65 us
  transfers between devices with their start and end apart: 14, of which 1 were waited for; matrix products, arithmetic and copies ran while one was open for 23% of the time, Pallas kernels for 0%

commit v1 on v0

--- a/solution.py
+++ b/solution.py
@@ -151,7 +151,7 @@
     grad_input = jnp.where(
         active, backward_sum.reshape(count, extent, extent, extent, channels), zero_f
     ).astype(jnp.bfloat16)
-    across_scans = lax.psum(kernel_grad, "dp")
+    across_scans = jnp.sum(lax.all_gather(kernel_grad, "dp"), axis=0)
     shard_rows = lax.psum_scatter(across_scans, "space", scatter_dimension=0, tiled=True)
     scale_factor = 1.0 / math.sqrt(scans_count * devices * count * extent**3)
     return (response[None], grad_input[None], shard_rows * scale_factor)

time: 263 us -> 294 us (1.12)
  waiting for transfers between devices: 4.08 us -> 61.4 us
  blocking collectives: 81.5 us -> 61.1 us
  local copies, waits for them, and re-layouts: 68.6 us -> 51.3 us
  between operations: 3 us -> 16.6 us
  other arithmetic: 25.1 us -> 14.9 us
  starting transfers between devices: 42.1 us -> 46.7 us
    all_gather x0 -> x1, waiting for transfers between devices: none -> 60.1 us  [per_device(): across_scans = jnp.sum(lax.all_gather(kernel_grad, 'dp'), axis=0)]
    psum x1 -> x0, blocking collectives: 17.2 us -> none  [per_device(): across_scans = lax.psum(kernel_grad, 'dp')]
    scatter x52, local copies, waits for them, and re-layouts: 25.9 us -> 9.15 us  [fill_rims(): padded = padded.at[whole + rim_slices(offset, extent)].set(picked)]
    select_n x26, other arithmetic: 17.2 us -> 2.39 us  [fill_rims(): picked = jnp.where((other >= 0)[:, None, None, None, None], picked, zero_bf)]
    unnamed x10, starting transfers between devices: 32.2 us -> 36.8 us
    reduce_sum x0 -> x1, other arithmetic: none -> 3.58 us  [per_device(): across_scans = jnp.sum(lax.all_gather(kernel_grad, 'dp'), axis=0)]
    unnamed x1, blocking collectives: 64.4 us -> 61.1 us
    unnamed x68 -> x85, local copies, waits for them, and re-layouts: 7.65 us -> 6.15 us
  transfers between devices with their start and end apart: 14 -> 15, of which waited for: 1 -> 2; matrix products, arithmetic and copies ran while one was open for 23% -> 11% of each run, Pallas kernels for 0% -> 0%
where the time goes in v1:
time: 294 us; the launch traced here: 290 us
  waiting for transfers between devices  61.4 us (21%)
  blocking collectives  61.1 us (21%)
  local copies, waits for them, and re-layouts  51.3 us (17%)
  starting transfers between devices  46.7 us (16%)
  matrix products  38 us (13%)
  between operations  16.6 us (6%)
  other arithmetic  14.9 us (5%)
    unnamed x1, blocking collectives  61.1 us
    all_gather x1, waiting for transfers between devices, per_device(): across_scans = jnp.sum(lax.all_gather(kernel_grad, 'dp'), axis=0)  60.1 us
    unnamed x10, starting transfers between devices  36.8 us
    gather x52, local copies, waits for them, and re-layouts, fill_rims(): picked = jnp.take(source, jnp.clip(local, 0, count - 1), axis=0)  29.1 us
    dot_general x27, matrix products, forward_each(): lax.dot_general(window, flat_g, (((0,), (0,)), ((), ())), preferred_eleme...  24.4 us
    scatter x52, local copies, waits for them, and re-layouts, fill_rims(): padded = padded.at[whole + rim_slices(offset, extent)].set(picked)  9.15 us
    dot_general x27, matrix products, backward_each(): lax.dot_general(window, weight[number], (((1,), (1,)), ((), ())), preferr...  7.74 us
    unnamed x85, local copies, waits for them, and re-layouts  6.15 us
  transfers between devices with their start and end apart: 15, of which 2 were waited for; matrix products, arithmetic and copies ran while one was open for 11% of the time, Pallas kernels for 0%

profile of v1, /device:TPU:6, one launch (start us, length us, event | category | flops | bytes accessed | tf_op | source)
XLA Modules:
  0.0 290.2 jit_solution(14889620193271688456)
XLA Ops:
  8.1 1.2 bitcast_select_fusion
  9.4 1.9 collective-permute-start.2
  11.3 3.8 %collective-permute-start = (bf16[1,2,8192]{2,1,0:T(2,128)(2,1)S(1)}, bf16[1,2,8192]{2,1,0:T(2,128)(2,1)S(1)}, u32[]{:S(2)}, u32[]{:S(2)}) collective-permute-start(bf16[1,2,8192]{2,1,0:T(2,128)(2,1)S(1)} %slice.2668), channel_id=1, source_target_pairs={{0,1},{1,2},{2,3},{3,4},{4,5},{5,6},{6,7},{7,8},{8,9},{9,10},{10,1... | collective-permute-start | bytes 98312 | tf_op jit(solution)/shard_map/ppermute | solution.py:27
  15.2 1.9 collective-permute-start.3
  17.1 2.2 collective-permute-start.1
  19.3 1.2 compare_reduce_fusion.19
  20.6 1.9 compare_reduce_fusion
  58.2 1.4 scatter.236
  59.6 1.4 scatter.239
  62.6 1.4 fusion.182
  64.0 2.5 fusion.181
  67.4 1.4 scatter.194
  68.8 1.4 scatter.195
  71.3 1.4 fusion.184
  73.6 0.9 fusion.26
  74.5 0.9 fusion.25
  76.3 0.9 fusion.23
  77.2 0.9 fusion.22
  79.0 0.9 fusion.20
  81.7 0.9 fusion.17
  82.6 0.9 fusion.16
  85.3 0.9 fusion.13
  87.1 0.9 fusion.11
  89.8 0.9 fusion.8
  90.7 0.9 fusion.7
  92.6 0.9 fusion.5
  93.5 0.9 fusion.4
  95.3 0.9 fusion.2
  96.2 0.9 fusion.1
  97.1 1.1 copy-done
  98.5 1.2 convolution_add_fusion.25
  107.6 0.9 convolution_add_fusion
  115.7 60.1 %all-gather.3.cloned.1.call-done = f32[13824,128]{1,0:T(8,128)} async-done(((f32[3456,128]{1,0:T(8,128)}), f32[13824,128]{1,0:T(8,128)}) %all-gather.3.cloned.1.call-update) | async-done | bytes 7077904 | tf_op jit(solution)/shard_map/all_gather | solution.py:154
  175.8 3.6 %reduce_sum.9 = f32[3456,128]{1,0:T(8,128)S(1)} reduce(f32[4,3456,128]{2,1,0:T(8,128)} %bitcast.753, f32[]{:T(128)} %constant.1488.clone.1), dimensions={0}, to_apply=%region_0.8 | reduce | flops 1327104 | bytes 8847364 | tf_op jit(solution)/shard_map/reduce_sum | solution.py:154
  179.4 61.1 %fusion = f32[64,128]{1,0:T(8,128)S(1)} fusion(f32[3456,128]{1,0:T(8,128)S(1)} %reduce_sum.9), kind=kCustom, calls=%all-reduce-scatter | all-reduce-scatter fusion | flops 524289 | bytes 1803264
  240.5 1.3 collective-permute-start.12
  241.8 4.2 %collective-permute-start.11 = (f32[64,128]{1,0:T(8,128)S(1)}, f32[64,128]{1,0:T(8,128)S(1)}, u32[]{:S(2)}, u32[]{:S(2)}) collective-permute-start(f32[64,128]{1,0:T(8,128)S(1)} %fusion), channel_id=1, source_target_pairs={{0,8},{1,9},{2,10},{3,11},{4,12},{5,13},{6,14},{7,15},{8,16},{9,17... | collective-permute-start | bytes 98312
  246.1 3.9 %collective-permute-start.10 = (f32[64,128]{1,0:T(8,128)S(1)}, f32[64,128]{1,0:T(8,128)S(1)}, u32[]{:S(2)}, u32[]{:S(2)}) collective-permute-start(f32[64,128]{1,0:T(8,128)S(1)} %fusion), channel_id=1, source_target_pairs={{0,7},{1,8},{2,9},{3,10},{4,11},{5,12},{6,13},{7,14},{8,15},{9,16}... | collective-permute-start | bytes 98312
  250.0 4.3 %collective-permute-start.9 = (f32[64,128]{1,0:T(8,128)S(1)}, f32[64,128]{1,0:T(8,128)S(1)}, u32[]{:S(2)}, u32[]{:S(2)}) collective-permute-start(f32[64,128]{1,0:T(8,128)S(1)} %fusion), channel_id=1, source_target_pairs={{0,6},{1,7},{2,8},{3,9},{4,10},{5,11},{6,12},{7,13},{8,14},{9,15},... | collective-permute-start | bytes 98312
  254.3 4.8 %collective-permute-start.13 = (f32[54,128]{1,0:T(8,128)S(1)}, f32[54,128]{1,0:T(8,128)S(1)}, u32[]{:S(2)}, u32[]{:S(2)}) collective-permute-start(f32[54,128]{1,0:T(8,128)S(1)} %slice.3039), channel_id=1, source_target_pairs={{0,10},{1,11},{2,12},{3,13},{4,14},{5,15},{6,16},{7,17},{8,18},{9,... | collective-permute-start | bytes 82952
  259.4 1.3 collective-permute-done.13
  260.7 2.1 collective-permute-start.8
  262.8 5.8 %collective-permute-start.7 = (f32[64,128]{1,0:T(8,128)S(1)}, f32[64,128]{1,0:T(8,128)S(1)}, u32[]{:S(2)}, u32[]{:S(2)}) collective-permute-start(f32[64,128]{1,0:T(8,128)S(1)} %fusion), channel_id=1, source_target_pairs={{0,4},{1,5},{2,6},{3,7},{4,8},{5,9},{6,10},{7,11},{8,12},{9,13},{1... | collective-permute-start | bytes 98312
  268.7 3.7 %collective-permute-start.6 = (f32[64,128]{1,0:T(8,128)S(1)}, f32[64,128]{1,0:T(8,128)S(1)}, u32[]{:S(2)}, u32[]{:S(2)}) collective-permute-start(f32[64,128]{1,0:T(8,128)S(1)} %fusion), channel_id=1, source_target_pairs={{0,3},{1,4},{2,5},{3,6},{4,7},{5,8},{6,9},{7,10},{8,11},{9,12},{10... | collective-permute-start | bytes 98312
  272.4 3.1 %collective-permute-start.5 = (f32[64,128]{1,0:T(8,128)S(1)}, f32[64,128]{1,0:T(8,128)S(1)}, u32[]{:S(2)}, u32[]{:S(2)}) collective-permute-start(f32[64,128]{1,0:T(8,128)S(1)} %fusion), channel_id=1, source_target_pairs={{0,2},{1,3},{2,4},{3,5},{4,6},{5,7},{6,8},{7,9},{8,10},{9,11},{10,... | collective-permute-start | bytes 98312
  275.5 3.5 %collective-permute-start.4 = (f32[64,128]{1,0:T(8,128)S(1)}, f32[64,128]{1,0:T(8,128)S(1)}, u32[]{:S(2)}, u32[]{:S(2)}) collective-permute-start(f32[64,128]{1,0:T(8,128)S(1)} %fusion), channel_id=1, source_target_pairs={{0,1},{1,2},{2,3},{3,4},{4,5},{5,6},{6,7},{7,8},{8,9},{9,10},{10,1... | collective-permute-start | bytes 98312
  279.0 2.0 select_convert_fusion
  281.0 1.7 concatenate.156
  (384 shorter events, 65.2 us)
Async XLA Ops:
  7.2 15.6 %copy-start.1 = (s32[1,2,26]{2,1,0:T(2,128)S(1)}, s32[1,2,26]{2,1,0:T(2,128)}, u32[]{:S(2)}) copy-start(s32[1,2,26]{2,1,0:T(2,128)} %param.125) | copy-start | bytes 628
  7.2 168.6 %all-gather.3.cloned.1.call-start = ((), (), s32[]{:S(2)}) async-start(), calls=%async_computation | async-start | bytes 8847360 | tf_op jit(solution)/shard_map/all_gather | solution.py:154
  9.4 26.6 %collective-permute-start.2 = (bf16[1,2,8192]{2,1,0:T(2,128)(2,1)S(1)}, bf16[1,2,8192]{2,1,0:T(2,128)(2,1)S(1)}, u32[]{:S(2)}, u32[]{:S(2)}) collective-permute-start(bf16[1,2,8192]{2,1,0:T(2,128)(2,1)S(1)} %slice.2775), channel_id=1, source_target_pairs={{0,1},{1,2},{2,3},{3,4},{4,5},{5,6},{6,7},{7,8},{8,9},{9,10},{10,1... | collective-permute-start | bytes 98312 | tf_op jit(solution)/shard_map/ppermute | solution.py:27
  11.3 24.7 %collective-permute-start = (bf16[1,2,8192]{2,1,0:T(2,128)(2,1)S(1)}, bf16[1,2,8192]{2,1,0:T(2,128)(2,1)S(1)}, u32[]{:S(2)}, u32[]{:S(2)}) collective-permute-start(bf16[1,2,8192]{2,1,0:T(2,128)(2,1)S(1)} %slice.2668), channel_id=1, source_target_pairs={{0,1},{1,2},{2,3},{3,4},{4,5},{5,6},{6,7},{7,8},{8,9},{9,10},{10,1... | collective-permute-start | bytes 98312 | tf_op jit(solution)/shard_map/ppermute | solution.py:27
  15.2 20.9 %collective-permute-start.3 = (bf16[1,2,8192]{2,1,0:T(2,128)(2,1)S(1)}, bf16[1,2,8192]{2,1,0:T(2,128)(2,1)S(1)}, u32[]{:S(2)}, u32[]{:S(2)}) collective-permute-start(bf16[1,2,8192]{2,1,0:T(2,128)(2,1)S(1)} %slice.2793), channel_id=1, source_target_pairs={{1,0},{2,1},{3,2},{4,3},{5,4},{6,5},{7,6},{8,7},{9,8},{10,9},{11,1... | collective-permute-start | bytes 98312 | tf_op jit(solution)/shard_map/ppermute | solution.py:30
  17.1 19.0 %collective-permute-start.1 = (bf16[1,2,8192]{2,1,0:T(2,128)(2,1)S(1)}, bf16[1,2,8192]{2,1,0:T(2,128)(2,1)S(1)}, u32[]{:S(2)}, u32[]{:S(2)}) collective-permute-start(bf16[1,2,8192]{2,1,0:T(2,128)(2,1)S(1)} %slice.2703), channel_id=1, source_target_pairs={{1,0},{2,1},{3,2},{4,3},{5,4},{6,5},{7,6},{8,7},{9,8},{10,9},{11,1... | collective-permute-start | bytes 98312 | tf_op jit(solution)/shard_map/ppermute | solution.py:30
  28.7 6.0 %copy-start.32 = (u32[256]{0:T(256)S(1)}, u32[256]{0:T(256)}, u32[]{:S(2)}) copy-start(u32[256]{0:T(256)} %constant.1500) | copy-start | bytes 3076
  97.1 1.2 copy-start
  97.1 2.6 copy-start.24
  97.1 2.9 copy-start.23
  98.5 1.7 copy-start.22
  99.7 1.0 copy-start.21
  100.0 1.0 copy-start.20
  100.2 1.0 copy-start.19
  100.7 1.0 copy-start.18
  101.0 1.0 copy-start.17
  101.2 1.0 copy-start.16
  101.7 1.0 copy-start.15
  101.9 1.0 copy-start.14
  102.5 1.0 copy-start.13
  102.9 1.0 copy-start.12
  103.2 1.0 copy-start.11
  103.4 1.0 copy-start.10
  103.9 1.0 copy-start.9
  104.2 1.0 copy-start.8
  104.4 1.0 copy-start.7
  104.9 1.0 copy-start.6
  105.1 1.0 copy-start.5
  105.4 1.0 copy-start.4
  105.8 1.0 copy-start.3
  106.1 1.0 copy-start.2
  107.1 1.4 copy-start.31
  107.4 1.4 copy-start.30
  107.6 1.4 copy-start.29
  108.5 1.0 copy-start.28
  108.8 1.0 copy-start.27
  109.0 1.0 copy-start.26
  109.5 1.0 copy-start.25
  240.5 22.3 %collective-permute-start.12 = (f32[64,128]{1,0:T(8,128)S(1)}, f32[64,128]{1,0:T(8,128)S(1)}, u32[]{:S(2)}, u32[]{:S(2)}) collective-permute-start(f32[64,128]{1,0:T(8,128)S(1)} %fusion), channel_id=1, source_target_pairs={{0,9},{1,10},{2,11},{3,12},{4,13},{5,14},{6,15},{7,16},{8,17},{9,1... | collective-permute-start | bytes 98312
  241.8 26.8 %collective-permute-start.11 = (f32[64,128]{1,0:T(8,128)S(1)}, f32[64,128]{1,0:T(8,128)S(1)}, u32[]{:S(2)}, u32[]{:S(2)}) collective-permute-start(f32[64,128]{1,0:T(8,128)S(1)} %fusion), channel_id=1, source_target_pairs={{0,8},{1,9},{2,10},{3,11},{4,12},{5,13},{6,14},{7,15},{8,16},{9,17... | collective-permute-start | bytes 98312
  246.1 26.3 %collective-permute-start.10 = (f32[64,128]{1,0:T(8,128)S(1)}, f32[64,128]{1,0:T(8,128)S(1)}, u32[]{:S(2)}, u32[]{:S(2)}) collective-permute-start(f32[64,128]{1,0:T(8,128)S(1)} %fusion), channel_id=1, source_target_pairs={{0,7},{1,8},{2,9},{3,10},{4,11},{5,12},{6,13},{7,14},{8,15},{9,16}... | collective-permute-start | bytes 98312
  250.0 25.5 %collective-permute-start.9 = (f32[64,128]{1,0:T(8,128)S(1)}, f32[64,128]{1,0:T(8,128)S(1)}, u32[]{:S(2)}, u32[]{:S(2)}) collective-permute-start(f32[64,128]{1,0:T(8,128)S(1)} %fusion), channel_id=1, source_target_pairs={{0,6},{1,7},{2,8},{3,9},{4,10},{5,11},{6,12},{7,13},{8,14},{9,15},... | collective-permute-start | bytes 98312
  254.3 6.4 %collective-permute-start.13 = (f32[54,128]{1,0:T(8,128)S(1)}, f32[54,128]{1,0:T(8,128)S(1)}, u32[]{:S(2)}, u32[]{:S(2)}) collective-permute-start(f32[54,128]{1,0:T(8,128)S(1)} %slice.3039), channel_id=1, source_target_pairs={{0,10},{1,11},{2,12},{3,13},{4,14},{5,15},{6,16},{7,17},{8,18},{9,... | collective-permute-start | bytes 82952
  260.7 20.3 %collective-permute-start.8 = (f32[64,128]{1,0:T(8,128)S(1)}, f32[64,128]{1,0:T(8,128)S(1)}, u32[]{:S(2)}, u32[]{:S(2)}) collective-permute-start(f32[64,128]{1,0:T(8,128)S(1)} %fusion), channel_id=1, source_target_pairs={{0,5},{1,6},{2,7},{3,8},{4,9},{5,10},{6,11},{7,12},{8,13},{9,14},{... | collective-permute-start | bytes 98312
  262.8 18.2 %collective-permute-start.7 = (f32[64,128]{1,0:T(8,128)S(1)}, f32[64,128]{1,0:T(8,128)S(1)}, u32[]{:S(2)}, u32[]{:S(2)}) collective-permute-start(f32[64,128]{1,0:T(8,128)S(1)} %fusion), channel_id=1, source_target_pairs={{0,4},{1,5},{2,6},{3,7},{4,8},{5,9},{6,10},{7,11},{8,12},{9,13},{1... | collective-permute-start | bytes 98312
  268.7 12.3 %collective-permute-start.6 = (f32[64,128]{1,0:T(8,128)S(1)}, f32[64,128]{1,0:T(8,128)S(1)}, u32[]{:S(2)}, u32[]{:S(2)}) collective-permute-start(f32[64,128]{1,0:T(8,128)S(1)} %fusion), channel_id=1, source_target_pairs={{0,3},{1,4},{2,5},{3,6},{4,7},{5,8},{6,9},{7,10},{8,11},{9,12},{10... | collective-permute-start | bytes 98312
  272.4 8.6 %collective-permute-start.5 = (f32[64,128]{1,0:T(8,128)S(1)}, f32[64,128]{1,0:T(8,128)S(1)}, u32[]{:S(2)}, u32[]{:S(2)}) collective-permute-start(f32[64,128]{1,0:T(8,128)S(1)} %fusion), channel_id=1, source_target_pairs={{0,2},{1,3},{2,4},{3,5},{4,6},{5,7},{6,8},{7,9},{8,10},{9,11},{10,... | collective-permute-start | bytes 98312
  275.5 5.5 %collective-permute-start.4 = (f32[64,128]{1,0:T(8,128)S(1)}, f32[64,128]{1,0:T(8,128)S(1)}, u32[]{:S(2)}, u32[]{:S(2)}) collective-permute-start(f32[64,128]{1,0:T(8,128)S(1)} %fusion), channel_id=1, source_target_pairs={{0,1},{1,2},{2,3},{3,4},{4,5},{5,6},{6,7},{7,8},{8,9},{9,10},{10,1... | collective-permute-start | bytes 98312
Sparse Core Ops, SparseCore 0:
  97.2 78.5 all-gather.2
